TPU v7x, 32 devices: a whole 2x2x4 slice. The times are simulated.
32 devices in a mesh: row: 4 (over y, x), col: 8 (over z, core).
Axes of the slice: x: 2, y: 2, z: 4, core: 2. Of those that a mesh axis runs over, the one named last changes fastest.
Arguments:
- integrals: bfloat16 [2880, 23040], P('row', 'col'), may hold values from -0.0390625 to 0.0390625
- amplitudes: bfloat16 [23040, 256], P('col', 'row'), may hold values from -6 to 6
Outputs:
- ladder: bfloat16 [256, 2880], P('col', 'row')
All inputs are finite; a program needn't handle non-finite values.
Results may differ from a plain program's by a relative error of at most 0.001.
Values may be sent and summed in bfloat16 or wider, within the bound.
A program may use at most 64 MiB of HBM per device.

v0:
```python
import jax
import jax.numpy as jnp
from jax import lax
from jax.sharding import PartitionSpec as P


def per_device(integrals, amplitudes):
    columns = lax.axis_size("col")
    gathered = lax.all_gather(amplitudes, "row", axis=1, tiled=True)
    local_rows = integrals.shape[0]
    row_count = (local_rows + columns - 1) // columns
    padded_rows = row_count * columns
    padded = jnp.pad(integrals, ((0, padded_rows - local_rows), (0, 0)))
    totals = lax.psum_scatter(
        jnp.dot(padded, gathered, preferred_element_type=jnp.float32),
        "col",
        scatter_dimension=0,
        tiled=True,
    ).astype(jnp.bfloat16)
    regrouped = lax.all_to_all(totals, "col", split_axis=1, concat_axis=0, tiled=True)
    return regrouped[:local_rows].T


def solution(mesh):
    in_specs = (P("row", "col"), P("col", "row"))
    out_specs = P("col", "row")
    return jax.shard_map(
        per_device, mesh=mesh, in_specs=in_specs, out_specs=out_specs, check_vma=False
    )
```

profile of v0, /device:TPU:0, one launch (start us, length us, event | category | flops | bytes accessed | tf_op | source)
XLA Modules:
  0.0 86.1 jit_solution(9630065998873702536)
XLA Ops:
  6.5 0.0 all-gather.2.cloned.1.call-start
  6.5 0.7 all-gather.2.cloned.1.call-update
  7.3 0.0 copy-start
  7.3 35.0 %all-gather.2.cloned.1.call-done = bf16[2880,256]{0,1:T(8,128)(2,1)} async-done(((bf16[2880,64]{0,1:T(8,128)(2,1)}), bf16[2880,256]{0,1:T(8,128)(2,1)}) %all-gather.2.cloned.1.call-update) | async-done | bytes 1474576 | tf_op jit(solution)/shard_map/all_gather | solution.py:9
  42.2 4.0 %fusion.1 = f32[720,256]{1,0:T(8,128)S(1)} fusion(bf16[720,2880]{1,0:T(8,128)(2,1)} %param.2, bf16[2880,256]{0,1:T(8,128)(2,1)} %all-gather.2.cloned.1.call-done), kind=kOutput, calls=%fused_computation.1 | convolution fusion | flops 1061683200 | bytes 6359040 | tf_op jit(solution)/shard_map/dot_general | solution.py:15
  46.2 20.7 %fusion = f32[96,256]{1,0:T(8,128)S(1)} fusion(f32[720,256]{1,0:T(8,128)S(1)} %fusion.1), kind=kCustom, calls=%all-reduce-scatter | all-reduce-scatter fusion | flops 196609 | bytes 836096
  67.0 1.3 %collective-permute-start = (bf16[42,256]{1,0:T(8,128)(2,1)S(1)}, bf16[42,256]{1,0:T(8,128)(2,1)S(1)}, u32[]{:S(2)}, u32[]{:S(2)}) collective-permute-start(bf16[42,256]{1,0:T(8,128)(2,1)S(1)} %slice), channel_id=1, source_target_pairs={{0,1},{1,2},{2,3},{3,4},{4,5},{5,6},{6,7},{8,9},{9,10},{10,11},{11... | collective-permute-start | bytes 64520
  68.3 0.0 copy-done
  68.3 0.6 dynamic-slice.4
  69.5 0.0 collective-permute-done
  69.5 0.3 concatenate
  69.8 0.1 copy.7
  70.0 8.5 %all_to_all.19 = bf16[90,8,32]{0,2,1:T(8,128)(2,1)S(1)} all-to-all(bf16[90,8,32]{0,2,1:T(8,128)(2,1)S(1)} %bitcast.10), channel_id=1, replica_groups=mesh['row'=4,'col'=8] {'col'}, dimensions={1} | all-to-all | bytes 92160 | tf_op jit(solution)/shard_map/all_to_all | solution.py:20
  78.5 0.7 all_to_all.17
  (3 shorter events, 0.1 us)
Async XLA Ops:
  6.5 35.7 %all-gather.2.cloned.1.call-start = ((), (), s32[]{:S(2)}) async-start(), calls=%async_computation.1 | async-start | bytes 1884160 | tf_op jit(solution)/shard_map/all_gather | solution.py:9
  7.3 61.0 %copy-start = (u32[32]{0:T(128)S(1)}, u32[32]{0:T(128)}, u32[]{:S(2)}) copy-start(u32[32]{0:T(128)} %constant.3) | copy-start | bytes 388
  67.0 2.6 %collective-permute-start = (bf16[42,256]{1,0:T(8,128)(2,1)S(1)}, bf16[42,256]{1,0:T(8,128)(2,1)S(1)}, u32[]{:S(2)}, u32[]{:S(2)}) collective-permute-start(bf16[42,256]{1,0:T(8,128)(2,1)S(1)} %slice), channel_id=1, source_target_pairs={{0,1},{1,2},{2,3},{3,4},{4,5},{5,6},{6,7},{8,9},{9,10},{10,11},{11... | collective-permute-start | bytes 64520
Sparse Core Ops, SparseCore 0:
  9.2 33.0 all-gather.1
where the time goes:
time: 86.3 us; the launch traced here: 86.1 us
  waiting for transfers between devices  35.7 us (41%)
  blocking collectives  29.2 us (34%)
  between operations  14.1 us (16%)
  matrix products  4 us (5%)
  local copies, waits for them, and re-layouts  1.76 us (2%)
  starting transfers between devices  1.29 us (1%)
    all_gather x1, waiting for transfers between devices, per_device(): gathered = lax.all_gather(amplitudes, 'row', axis=1, tiled=True)  35 us
    unnamed x1, blocking collectives  20.7 us
    all_to_all x1, blocking collectives, per_device(): lax.all_to_all(totals, 'col', split_axis=1, concat_axis=0, tiled=True)  8.52 us
    dot_general x1, matrix products, per_device(): jnp.dot(padded, gathered, preferred_element_type=jnp.float32)  4 us
  transfers between devices with their start and end apart: 2, of which 1 were waited for; matrix products, arithmetic and copies ran while one was open for 1% of the time, Pallas kernels for 0%

commit v1 on v0

v1 whole, which is shorter than its diff:
```python
import functools

import jax
import jax.numpy as jnp
from jax import lax
from jax.experimental import pallas as pl
from jax.experimental.pallas import tpu as pltpu
from jax.sharding import PartitionSpec as P

MESH = pl.DeviceIdType.MESH
NT = (((1,), (1,)), ((), ()))


def cuts_of(size, pieces, step):
    width = -(-size // (pieces * step)) * step
    return [(at, min(width, size - at)) for at in range(0, size, width)]


def ladder_kernel(chips, cuts, v_ref, t_ref, out_ref, v, t, parts, swap, summed, landed,
                  v_sem, t_sem, own_send, own_recv, far_send, far_recv,
                  swap_send, swap_recv, line_send, line_recv):
    half = t_ref.shape[0] // 2
    r, c = lax.axis_index("row"), lax.axis_index("col")
    z, core = c // 2, c % 2
    rx = r + 1 - 2 * (r % 2)
    ry = r + 2 - 4 * (r // 2)
    rd = 3 - r
    other = 1 - core

    def rows_of(h):
        return pl.ds(h * half, half)

    t_copy = pltpu.make_async_copy(t_ref, t.at[0], t_sem)
    t_copy.start()
    v_copies = []
    for i, (at, width) in enumerate(cuts):
        copy = pltpu.make_async_copy(v_ref.at[:, pl.ds(at, width)], v.at[:, pl.ds(at, width)], v_sem.at[i])
        copy.start()
        v_copies.append(copy)

    barrier = pltpu.get_barrier_semaphore()
    pl.semaphore_signal(barrier, inc=1, device_id={"row": rx}, device_id_type=MESH)
    pl.semaphore_signal(barrier, inc=1, device_id={"row": ry}, device_id_type=MESH)
    pl.semaphore_signal(barrier, inc=1, device_id={"col": 2 * z + other}, device_id_type=MESH)
    for step in range(1, chips):
        peer = lax.rem(z + step, chips)
        pl.semaphore_signal(barrier, inc=1, device_id={"col": 2 * peer + core}, device_id_type=MESH)
    pl.semaphore_wait(barrier, chips + 2)

    own = []
    for i, (h, slot, to) in enumerate(((0, 1, rx), (1, 1, ry), (1, 2, rx), (0, 2, ry))):
        copy = pltpu.make_async_remote_copy(
            src_ref=t_ref.at[rows_of(h)], dst_ref=t.at[slot, rows_of(h)],
            send_sem=own_send.at[i], recv_sem=own_recv.at[i], device_id={"row": to}, device_id_type=MESH)
        copy.start()
        own.append(copy)

    def multiply(slot, at, width):
        return lax.dot_general(t[slot, :, at:at + width], v[:, at:at + width], NT, preferred_element_type=jnp.float32)

    def swap_start(slot):
        copy = pltpu.make_async_remote_copy(
            src_ref=parts.at[slot, rows_of(other)], dst_ref=swap.at[slot],
            send_sem=swap_send.at[slot], recv_sem=swap_recv.at[slot],
            device_id={"col": 2 * z + other}, device_id_type=MESH)
        copy.start()
        return copy

    def goal(slot):
        first, second = ((r, r), (rx, ry), (ry, rx), (rd, rd))[slot]
        return first * other + second * core

    def line_copy(slot):
        return pltpu.make_async_remote_copy(
            src_ref=summed.at[slot], dst_ref=landed.at[z],
            send_sem=line_send.at[slot], recv_sem=line_recv.at[z],
            device_id={"col": 2 * goal(slot) + core}, device_id_type=MESH)

    def swap_finish(slot, copy):
        copy.wait_recv()
        total = parts[slot, rows_of(core)] + swap[slot]

        @pl.when(goal(slot) == z)
        def _():
            landed[z] = total

        @pl.when(goal(slot) != z)
        def _():
            summed[slot] = total
            line_copy(slot).start()

    t_copy.wait()
    for i, (at, width) in enumerate(cuts):
        v_copies[i].wait()
        term = multiply(0, at, width)
        parts[0] = term if i == 0 else parts[0] + term
    swaps = [swap_start(0)]

    own[0].wait_recv()
    own[1].wait_recv()
    far = []
    for i, (at, width) in enumerate(cuts):
        for h, to in ((0, ry), (1, rx)):
            where = (rows_of(h), pl.ds(at, width))
            copy = pltpu.make_async_remote_copy(
                src_ref=t.at[(1, *where)], dst_ref=t.at[(3, *where)],
                send_sem=far_send.at[i, h], recv_sem=far_recv.at[i, h], device_id={"row": to}, device_id_type=MESH)
            copy.start()
            far.append(copy)

    swap_finish(0, swaps[0])
    parts[1] = multiply(1, 0, t_ref.shape[1])
    swaps.append(swap_start(1))

    own[2].wait_recv()
    own[3].wait_recv()
    parts[2] = multiply(2, 0, t_ref.shape[1])
    swaps.append(swap_start(2))
    swap_finish(1, swaps[1])
    swap_finish(2, swaps[2])

    for i, (at, width) in enumerate(cuts):
        far[2 * i].wait_recv()
        far[2 * i + 1].wait_recv()
        term = multiply(3, at, width)
        parts[3] = term if i == 0 else parts[3] + term
    swaps.append(swap_start(3))
    swap_finish(3, swaps[3])

    for source in range(chips):
        @pl.when(z != source)
        def _():
            pltpu.make_async_copy(landed.at[source], landed.at[source], line_recv.at[source]).wait()
    total = landed[0]
    for source in range(1, chips):
        total = total + landed[source]
    out_ref[...] = total.astype(out_ref.dtype)

    for copy in own + far + swaps:
        copy.wait_send()
    for slot in range(4):
        @pl.when(goal(slot) != z)
        def _():
            line_copy(slot).wait_send()


def ladder_on_chips(integrals, amplitudes):
    chips = lax.axis_size("col") // 2
    blocks = amplitudes.T
    pairs, depth = blocks.shape
    rows = integrals.shape[0]
    half = pairs // 2
    cuts = cuts_of(depth, 4, 256)
    f32 = jnp.float32
    dma = pltpu.SemaphoreType.DMA
    return pl.pallas_call(
        functools.partial(ladder_kernel, chips, cuts),
        out_shape=jax.ShapeDtypeStruct((half, rows), jnp.bfloat16),
        in_specs=[pl.BlockSpec(memory_space=pl.ANY)] * 2,
        out_specs=pl.BlockSpec(memory_space=pltpu.VMEM),
        scratch_shapes=[
            pltpu.VMEM((rows, depth), jnp.bfloat16),
            pltpu.VMEM((4, pairs, depth), jnp.bfloat16),
            pltpu.VMEM((4, pairs, rows), f32),
            pltpu.VMEM((4, half, rows), f32),
            pltpu.VMEM((4, half, rows), f32),
            pltpu.VMEM((chips, half, rows), f32),
            dma((len(cuts),)), dma,
            dma((4,)), dma((4,)),
            dma((len(cuts), 2)), dma((len(cuts), 2)),
            dma((4,)), dma((4,)),
            dma((4,)), dma((chips,)),
        ],
        compiler_params=pltpu.CompilerParams(
            collective_id=0, has_side_effects=True, vmem_limit_bytes=48 * 1024 * 1024),
    )(integrals, blocks)


def per_device(integrals, amplitudes):
    columns = lax.axis_size("col")
    if lax.axis_size("row") == 4 and columns == 8:
        return ladder_on_chips(integrals, amplitudes)
    gathered = lax.all_gather(amplitudes, "row", axis=1, tiled=True)
    product = lax.dot_general(
        gathered, integrals, (((0,), (1,)), ((), ())), preferred_element_type=jnp.float32)
    return lax.psum_scatter(product, "col", scatter_dimension=0, tiled=True).astype(jnp.bfloat16)


def solution(mesh):
    in_specs = (P("row", "col"), P("col", "row"))
    out_specs = P("col", "row")
    return jax.shard_map(
        per_device, mesh=mesh, in_specs=in_specs, out_specs=out_specs, check_vma=False
    )
```

time: 86.3 us -> 31.6 us (0.37)
  the two profiles are of different devices: /device:TPU:0 before, /device:TPU:6 now
where the time goes in v1:
time: 31.6 us; the launch traced here: 31.4 us
  Pallas kernels  27.6 us (87%)
  local copies, waits for them, and re-layouts  3.81 us (12%)
    pallas_call x1, Pallas kernels, ladder_on_chips(): pl.pallas_call(functools.partial(ladder_kernel, chips, cuts), out_shape=j...  27.6 us
    unnamed x5, local copies, waits for them, and re-layouts  3.81 us

profile of v1, /device:TPU:6, one launch (start us, length us, event | category | flops | bytes accessed | tf_op | source)
XLA Modules:
  0.0 31.4 jit_solution(15836854335866315946)
XLA Ops:
  0.0 0.0 copy-start
  0.0 2.2 %copy-done = bf16[720,2880]{1,0:T(8,128)(2,1)S(1)} copy-done((bf16[720,2880]{1,0:T(8,128)(2,1)S(1)}, bf16[720,2880]{1,0:T(8,128)(2,1)}, u32[]{:S(2)}) %copy-start) | copy-done | bytes 4147224
  2.2 0.0 copy-start.1
  2.2 1.0 %copy-done.1 = bf16[2880,64]{0,1:T(8,128)(2,1)S(1)} copy-done((bf16[2880,64]{0,1:T(8,128)(2,1)S(1)}, bf16[2880,64]{0,1:T(8,128)(2,1)}, u32[]{:S(2)}) %copy-start.1) | copy-done | bytes 368664
  3.2 27.6 %shard_map.28 = bf16[32,720]{1,0:T(8,128)(2,1)S(1)} custom-call(bf16[720,2880]{1,0:T(8,128)(2,1)S(1)} %copy-done, bf16[64,2880]{1,0:T(8,128)(2,1)S(1)} %bitcast.1), custom_call_target="tpu_custom_call" | custom-call | tf_op jit(solution)/shard_map/pallas_call | solution.py:156
  30.8 0.6 %copy.4 = bf16[32,720]{1,0:T(8,128)(2,1)} copy(bf16[32,720]{1,0:T(8,128)(2,1)S(1)} %shard_map.28) | data formatting | bytes 92160
Async XLA Ops:
  0.0 2.2 %copy-start = (bf16[720,2880]{1,0:T(8,128)(2,1)S(1)}, bf16[720,2880]{1,0:T(8,128)(2,1)}, u32[]{:S(2)}) copy-start(bf16[720,2880]{1,0:T(8,128)(2,1)} %v_ref.1) | copy-start | bytes 12441604
  2.2 1.0 %copy-start.1 = (bf16[2880,64]{0,1:T(8,128)(2,1)S(1)}, bf16[2880,64]{0,1:T(8,128)(2,1)}, u32[]{:S(2)}) copy-start(bf16[2880,64]{0,1:T(8,128)(2,1)} %param.3) | copy-start | bytes 1105924

commit v2 on v1

v2 whole, which is shorter than its diff:
```python
import functools

import jax
import jax.numpy as jnp
from jax import lax
from jax.experimental import pallas as pl
from jax.experimental.pallas import tpu as pltpu
from jax.sharding import PartitionSpec as P

MESH = pl.DeviceIdType.MESH
NT = (((1,), (1,)), ((), ()))


def cuts_of(size, pieces, step):
    width = -(-size // (pieces * step)) * step
    return [(at, min(width, size - at)) for at in range(0, size, width)]


def ladder_kernel(chips, cuts, v_ref, t_ref, out_ref, v, t, parts, swap, summed, landed,
                  v_sem, t_sem, near_send, near_recv, far_send, far_recv, late_send, late_recv, last_send, last_recv,
                  swap_send, swap_recv, line_send, line_recv):
    depth = t_ref.shape[1]
    half = t_ref.shape[0] // 2
    part = half // 2
    r, c = lax.axis_index("row"), lax.axis_index("col")
    z, core = c // 2, c % 2
    rx = r + 1 - 2 * (r % 2)
    ry = r + 2 - 4 * (r // 2)
    rd = 3 - r
    other = 1 - core
    own = (0, half, (r, r), 0)
    near = (2 * half, half, (rx, ry), 0)
    far = [(4 * half + 4 * part * j, part, (rd, rd), part * j) for j in range(2)]
    late = [(4 * half + 4 * part * j + 2 * part, part, (ry, rx), part * j) for j in range(2)]
    slots = [own, near, far[0], late[0], far[1], late[1]]

    t_copy = pltpu.make_async_copy(t_ref, t.at[pl.ds(0, 2 * half)], t_sem)
    t_copy.start()
    v_copies = []
    for i, (at, width) in enumerate(cuts):
        copy = pltpu.make_async_copy(v_ref.at[:, pl.ds(at, width)], v.at[:, pl.ds(at, width)], v_sem.at[i])
        copy.start()
        v_copies.append(copy)

    barrier = pltpu.get_barrier_semaphore()
    pl.semaphore_signal(barrier, inc=1, device_id={"row": rx}, device_id_type=MESH)
    pl.semaphore_signal(barrier, inc=1, device_id={"row": ry}, device_id_type=MESH)
    pl.semaphore_signal(barrier, inc=1, device_id={"col": 2 * z + other}, device_id_type=MESH)
    for step in range(1, chips):
        peer = lax.rem(z + step, chips)
        pl.semaphore_signal(barrier, inc=1, device_id={"col": 2 * peer + core}, device_id_type=MESH)
    pl.semaphore_wait(barrier, chips + 2)

    def send(source, target, to, sems):
        copy = pltpu.make_async_remote_copy(
            src_ref=source, dst_ref=target, send_sem=sems[0], recv_sem=sems[1],
            device_id={"row": to}, device_id_type=MESH)
        copy.start()
        return copy

    def at_rows(first, count):
        return t.at[pl.ds(first, count)]

    near_copies = []
    for j in range(2):
        for h, to in ((0, rx), (1, ry)):
            near_copies.append(send(
                t_ref.at[pl.ds(h * half + j * part, part)], at_rows(near[0] + h * half + j * part, part), to,
                (near_send.at[j, h], near_recv.at[j, h])))

    def relay(j):
        copies = []
        for h, to in ((0, ry), (1, rx)):
            copies.append(send(
                at_rows(near[0] + h * half + j * part, part), at_rows(far[j][0] + h * part, part), to,
                (far_send.at[j, h], far_recv.at[j, h])))
        return copies

    def multiply(slot, at, width, several=1):
        first, count = slot[0], 2 * slot[1] * several
        return lax.dot_general(
            t[first:first + count, at:at + width], v[:, at:at + width], NT, preferred_element_type=jnp.float32)

    def swap_start(i):
        first, count, _, _ = slots[i]
        copy = pltpu.make_async_remote_copy(
            src_ref=parts.at[pl.ds(first + other * count, count)], dst_ref=swap.at[pl.ds(first // 2, count)],
            send_sem=swap_send.at[i], recv_sem=swap_recv.at[i],
            device_id={"col": 2 * z + other}, device_id_type=MESH)
        copy.start()
        return copy

    def goal(i):
        one, two = slots[i][2]
        return one * other + two * core

    def line_copy(i):
        first, count, _, place = slots[i]
        return pltpu.make_async_remote_copy(
            src_ref=summed.at[pl.ds(first // 2, count)], dst_ref=landed.at[z, pl.ds(place, count)],
            send_sem=line_send.at[i], recv_sem=line_recv.at[z],
            device_id={"col": 2 * goal(i) + core}, device_id_type=MESH)

    def swap_finish(i, copy):
        first, count, _, place = slots[i]
        copy.wait_recv()
        total = parts[pl.ds(first + core * count, count)] + swap[first // 2:first // 2 + count]

        @pl.when(goal(i) == z)
        def _():
            landed[z, place:place + count] = total

        @pl.when(goal(i) != z)
        def _():
            summed[first // 2:first // 2 + count] = total
            line_copy(i).start()

    def store(i, value):
        first, count = slots[i][0], 2 * slots[i][1]
        parts[first:first + count] = value

    def wait(copies):
        for copy in copies:
            copy.wait_recv()

    t_copy.wait()
    total = None
    for i, (at, width) in enumerate(cuts):
        v_copies[i].wait()
        term = multiply(own, at, width)
        total = term if total is None else total + term
    store(0, total)
    swaps = [swap_start(0)]

    wait(near_copies[:2])
    far_copies = relay(0)
    late_copies = []
    for h, to in ((1, rx), (0, ry)):
        late_copies.append(send(
            t_ref.at[pl.ds(h * half, part)], at_rows(late[0][0] + h * part, part), to,
            (late_send.at[h], late_recv.at[h])))
    swap_finish(0, swaps[0])

    wait(near_copies[2:])
    far_copies += relay(1)
    last_copies = []
    for i, (at, width) in enumerate(cuts):
        for h, to in ((1, rx), (0, ry)):
            last_copies.append(send(
                t_ref.at[pl.ds(h * half + part, part), pl.ds(at, width)],
                t.at[pl.ds(late[1][0] + h * part, part), pl.ds(at, width)], to,
                (last_send.at[i, h], last_recv.at[i, h])))
    store(1, multiply(near, 0, depth))
    swaps.append(swap_start(1))

    wait(far_copies[:2])
    swap_finish(1, swaps[1])
    wait(late_copies)
    both = multiply(far[0], 0, depth, several=2)
    store(2, both[:2 * part])
    store(3, both[2 * part:])
    swaps.append(swap_start(2))
    swaps.append(swap_start(3))

    wait(far_copies[2:])
    store(4, multiply(far[1], 0, depth))
    swaps.append(swap_start(4))
    swap_finish(2, swaps[2])
    swap_finish(3, swaps[3])

    total = None
    for i, (at, width) in enumerate(cuts):
        wait(last_copies[2 * i:2 * i + 2])
        term = multiply(late[1], at, width)
        total = term if total is None else total + term
        if i == len(cuts) - 2:
            swap_finish(4, swaps[4])
    store(5, total)
    swaps.append(swap_start(5))
    swap_finish(5, swaps[5])

    for source in range(chips):
        @pl.when(z != source)
        def _():
            pltpu.make_async_copy(landed.at[source], landed.at[source], line_recv.at[source]).wait()
    total = landed[0]
    for source in range(1, chips):
        total = total + landed[source]
    out_ref[...] = total.astype(out_ref.dtype)

    for copy in near_copies + far_copies + late_copies + last_copies + swaps:
        copy.wait_send()
    for i in range(len(slots)):
        @pl.when(goal(i) != z)
        def _():
            line_copy(i).wait_send()


def ladder_on_chips(integrals, amplitudes):
    chips = lax.axis_size("col") // 2
    blocks = amplitudes.T
    pairs, depth = blocks.shape
    rows = integrals.shape[0]
    half = pairs // 2
    cuts = cuts_of(depth, 4, 256)
    f32 = jnp.float32
    dma = pltpu.SemaphoreType.DMA
    return pl.pallas_call(
        functools.partial(ladder_kernel, chips, cuts),
        out_shape=jax.ShapeDtypeStruct((half, rows), jnp.bfloat16),
        in_specs=[pl.BlockSpec(memory_space=pl.ANY)] * 2,
        out_specs=pl.BlockSpec(memory_space=pltpu.VMEM),
        scratch_shapes=[
            pltpu.VMEM((rows, depth), jnp.bfloat16),
            pltpu.VMEM((4 * pairs, depth), jnp.bfloat16),
            pltpu.VMEM((4 * pairs, rows), f32),
            pltpu.VMEM((2 * pairs, rows), f32),
            pltpu.VMEM((2 * pairs, rows), f32),
            pltpu.VMEM((chips, half, rows), f32),
            dma((len(cuts),)), dma,
            dma((2, 2)), dma((2, 2)),
            dma((2, 2)), dma((2, 2)),
            dma((2,)), dma((2,)),
            dma((len(cuts), 2)), dma((len(cuts), 2)),
            dma((6,)), dma((6,)),
            dma((6,)), dma((chips,)),
        ],
        compiler_params=pltpu.CompilerParams(
            collective_id=0, has_side_effects=True, vmem_limit_bytes=67043328),
    )(integrals, blocks)


def per_device(integrals, amplitudes):
    columns = lax.axis_size("col")
    if lax.axis_size("row") == 4 and columns == 8:
        return ladder_on_chips(integrals, amplitudes)
    gathered = lax.all_gather(amplitudes, "row", axis=1, tiled=True)
    product = lax.dot_general(
        gathered, integrals, (((0,), (1,)), ((), ())), preferred_element_type=jnp.float32)
    return lax.psum_scatter(product, "col", scatter_dimension=0, tiled=True).astype(jnp.bfloat16)


def solution(mesh):
    in_specs = (P("row", "col"), P("col", "row"))
    out_specs = P("col", "row")
    return jax.shard_map(
        per_device, mesh=mesh, in_specs=in_specs, out_specs=out_specs, check_vma=False
    )
```

time: 31.6 us -> 28.8 us (0.911)
  the two profiles are of different devices: /device:TPU:6 before, /device:TPU:4 now
where the time goes in v2:
time: 28.8 us; the launch traced here: 28.6 us
  Pallas kernels  27.2 us (94%)
  local copies, waits for them, and re-layouts  1.42 us (5%)
    pallas_call x1, Pallas kernels, ladder_on_chips(): pl.pallas_call(functools.partial(ladder_kernel, chips, cuts), out_shape=j...  27.2 us
    unnamed x1, local copies, waits for them, and re-layouts  1.42 us

profile of v2, /device:TPU:4, one launch (start us, length us, event | category | flops | bytes accessed | tf_op | source)
XLA Modules:
  0.0 28.6 jit_solution(10556871475115213936)
XLA Ops:
  0.0 27.2 %shard_map.28 = bf16[32,720]{1,0:T(8,128)(2,1)} custom-call(bf16[720,2880]{1,0:T(8,128)(2,1)} %v_ref.1, bf16[64,2880]{1,0:T(8,128)(2,1)} %bitcast.1), custom_call_target="tpu_custom_call" | custom-call | tf_op jit(solution)/shard_map/pallas_call | solution.py:208
  27.2 1.4 %copy.4 = bf16[32,720]{1,0:T(8,128)(2,1)} copy(bf16[32,720]{1,0:T(8,128)(2,1)} %shard_map.28) | data formatting | bytes 92160

commit v3 on v2

--- a/solution.py
+++ b/solution.py
@@ -30,9 +30,9 @@
     other = 1 - core
     own = (0, half, (r, r), 0)
     near = (2 * half, half, (rx, ry), 0)
-    far = [(4 * half + 4 * part * j, part, (rd, rd), part * j) for j in range(2)]
-    late = [(4 * half + 4 * part * j + 2 * part, part, (ry, rx), part * j) for j in range(2)]
-    slots = [own, near, far[0], late[0], far[1], late[1]]
+    far = [(4 * half + 2 * part * j, part, (rd, rd), part * j) for j in range(2)]
+    late = (6 * half, half, (ry, rx), 0)
+    slots = [own, near, *far, late]
 
     t_copy = pltpu.make_async_copy(t_ref, t.at[pl.ds(0, 2 * half)], t_sem)
     t_copy.start()
@@ -76,8 +76,8 @@
                 (far_send.at[j, h], far_recv.at[j, h])))
         return copies
 
-    def multiply(slot, at, width, several=1):
-        first, count = slot[0], 2 * slot[1] * several
+    def multiply(slot, at, width):
+        first, count = slot[0], 2 * slot[1]
         return lax.dot_general(
             t[first:first + count, at:at + width], v[:, at:at + width], NT, preferred_element_type=jnp.float32)
 
@@ -134,50 +134,45 @@
 
     wait(near_copies[:2])
     far_copies = relay(0)
+    swap_finish(0, swaps[0])
+    wait(near_copies[2:])
+    far_copies += relay(1)
     late_copies = []
     for h, to in ((1, rx), (0, ry)):
         late_copies.append(send(
-            t_ref.at[pl.ds(h * half, part)], at_rows(late[0][0] + h * part, part), to,
+            t_ref.at[pl.ds(h * half, part)], at_rows(late[0] + h * half, part), to,
             (late_send.at[h], late_recv.at[h])))
-    swap_finish(0, swaps[0])
-
-    wait(near_copies[2:])
-    far_copies += relay(1)
     last_copies = []
     for i, (at, width) in enumerate(cuts):
         for h, to in ((1, rx), (0, ry)):
             last_copies.append(send(
                 t_ref.at[pl.ds(h * half + part, part), pl.ds(at, width)],
-                t.at[pl.ds(late[1][0] + h * part, part), pl.ds(at, width)], to,
+                t.at[pl.ds(late[0] + h * half + part, part), pl.ds(at, width)], to,
                 (last_send.at[i, h], last_recv.at[i, h])))
     store(1, multiply(near, 0, depth))
     swaps.append(swap_start(1))
 
     wait(far_copies[:2])
+    store(2, multiply(far[0], 0, depth))
+    swaps.append(swap_start(2))
     swap_finish(1, swaps[1])
+
+    wait(far_copies[2:])
+    store(3, multiply(far[1], 0, depth))
+    swaps.append(swap_start(3))
+    swap_finish(2, swaps[2])
+
     wait(late_copies)
-    both = multiply(far[0], 0, depth, several=2)
-    store(2, both[:2 * part])
-    store(3, both[2 * part:])
-    swaps.append(swap_start(2))
-    swaps.append(swap_start(3))
-
-    wait(far_copies[2:])
-    store(4, multiply(far[1], 0, depth))
+    total = None
+    for i, (at, width) in enumerate(cuts):
+        wait(last_copies[2 * i:2 * i + 2])
+        term = multiply(late, at, width)
+        total = term if total is None else total + term
+        if i == 0:
+            swap_finish(3, swaps[3])
+    store(4, total)
     swaps.append(swap_start(4))
-    swap_finish(2, swaps[2])
-    swap_finish(3, swaps[3])
-
-    total = None
-    for i, (at, width) in enumerate(cuts):
-        wait(last_copies[2 * i:2 * i + 2])
-        term = multiply(late[1], at, width)
-        total = term if total is None else total + term
-        if i == len(cuts) - 2:
-            swap_finish(4, swaps[4])
-    store(5, total)
-    swaps.append(swap_start(5))
-    swap_finish(5, swaps[5])
+    swap_finish(4, swaps[4])
 
     for source in range(chips):
         @pl.when(z != source)
@@ -202,7 +197,7 @@
     pairs, depth = blocks.shape
     rows = integrals.shape[0]
     half = pairs // 2
-    cuts = cuts_of(depth, 4, 256)
+    cuts = cuts_of(depth, 2, 256)
     f32 = jnp.float32
     dma = pltpu.SemaphoreType.DMA
     return pl.pallas_call(
@@ -222,8 +217,8 @@
             dma((2, 2)), dma((2, 2)),
             dma((2,)), dma((2,)),
             dma((len(cuts), 2)), dma((len(cuts), 2)),
-            dma((6,)), dma((6,)),
-            dma((6,)), dma((chips,)),
+            dma((5,)), dma((5,)),
+            dma((5,)), dma((chips,)),
         ],
         compiler_params=pltpu.CompilerParams(
             collective_id=0, has_side_effects=True, vmem_limit_bytes=67043328),

time: 28.8 us -> 28.3 us (0.983)
  Pallas kernels: 27.2 us -> 26.7 us
    pallas_call x1, Pallas kernels: 27.2 us -> 26.7 us  [ladder_on_chips(): pl.pallas_call(functools.partial(ladder_kernel, chips, cuts), out_shape=j...]
where the time goes in v3:
time: 28.3 us; the launch traced here: 28.1 us
  Pallas kernels  26.7 us (94%)
  local copies, waits for them, and re-layouts  1.42 us (5%)
    pallas_call x1, Pallas kernels, ladder_on_chips(): pl.pallas_call(functools.partial(ladder_kernel, chips, cuts), out_shape=j...  26.7 us
    unnamed x1, local copies, waits for them, and re-layouts  1.42 us

profile of v3, /device:TPU:4, one launch (start us, length us, event | category | flops | bytes accessed | tf_op | source)
XLA Modules:
  0.0 28.1 jit_solution(1346194651075714808)
XLA Ops:
  0.0 26.7 %shard_map.28 = bf16[32,720]{1,0:T(8,128)(2,1)} custom-call(bf16[720,2880]{1,0:T(8,128)(2,1)} %v_ref.1, bf16[64,2880]{1,0:T(8,128)(2,1)} %bitcast.1), custom_call_target="tpu_custom_call" | custom-call | tf_op jit(solution)/shard_map/pallas_call | solution.py:203
  26.7 1.4 %copy.4 = bf16[32,720]{1,0:T(8,128)(2,1)} copy(bf16[32,720]{1,0:T(8,128)(2,1)} %shard_map.28) | data formatting | bytes 92160
